TPU v7x, 32 devices: a whole 2x2x4 slice. The times are simulated.
32 devices in a mesh: az: 4 (over z), rad: 2 (over x), ax: 4 (over y, core).
Axes of the slice: x: 2, y: 2, z: 4, core: 2. Of those that a mesh axis runs over, the one named last changes fastest.
Arguments:
- cycle: float32 [4, 5, 512, 4096], P(None, None, ('rad', 'ax'), 'az'), may hold values from -6 to 6
- field: float32 [5, 64, 8, 4096], P(None, 'rad', 'ax', 'az'), may hold values from -6 to 6
- shift: int32 [1], replicated, may hold values from 0 to 4095
- owner: int32 [64, 8], P('rad', 'ax'), may hold values 0 or 1
Outputs:
- field_next: float32 [5, 64, 8, 4096], P(None, 'rad', 'ax', 'az')
- shifted_cycle: float32 [4, 5, 512, 4096], P(None, None, ('rad', 'ax'), 'az')
All inputs are finite; a program needn't handle non-finite values. No bound on the sum of `owner` on one device may be relied on, other than what follows from the above.
Results may differ from a plain program's by a relative error of at most 0.00007.
Values sent between devices are 32-bit elements; how exact they have to be, the bound alone decides.
A program may use at most 192 MiB of HBM per device.

v0:
```python
import math
import jax
import jax.numpy as jnp
from jax import lax
from jax.sharding import PartitionSpec as P

KR = 8
LAYER_WEIGHTS = (0.4, 0.3, 0.2, 0.1)
AXIAL_SPEEDS = (0.35, 0.2, 0.3, 0.25, 0.4)
DIFFUSION = 0.15
SWIRL_SPEED = 0.1


def padded(array, sides, width):
    for axis, dim in sides:
        devices, length = (lax.axis_size(axis), array.shape[dim])
        up = [(i, (i + 1) % devices) for i in range(devices - 1)]
        down = [(j, i) for i, j in up]
        last = lax.slice_in_dim(array, length - width, length, axis=dim)
        leading = lax.slice_in_dim(array, 0, width, axis=dim)
        before = lax.ppermute(last, axis, up)
        after = lax.ppermute(leading, axis, down)
        array = jnp.concatenate([before, array, after], axis=dim)
    return array


def turn_table(first, second, modulus):
    product = jnp.remainder(first[:, None] * second[None, :], modulus).astype(jnp.float32)
    angle = product * (2.0 * math.pi / modulus)
    return (jnp.cos(angle), jnp.sin(angle))


def spectral_shift(rows, shift_value):
    count, length = rows.shape
    half_bits = (length.bit_length() - 1) // 2
    outer = 2**half_bits
    inner = length // outer
    hp = lax.Precision.HIGHEST
    outer_index = jnp.arange(outer, dtype=jnp.int32)
    inner_index = jnp.arange(inner, dtype=jnp.int32)
    cos_outer, sin_outer = turn_table(outer_index, outer_index, outer)
    cos_inner, sin_inner = turn_table(inner_index, inner_index, inner)
    cos_twist, sin_twist = turn_table(outer_index, inner_index, length)
    grid = rows.reshape(count, outer, inner)
    section_re = jnp.einsum("bpq,pk->bkq", grid, cos_outer, precision=hp)
    section_im = -jnp.einsum("bpq,pk->bkq", grid, sin_outer, precision=hp)
    twist_re = section_re * cos_twist + section_im * sin_twist
    twist_im = section_im * cos_twist - section_re * sin_twist
    spec_re = jnp.einsum("bkq,qm->bkm", twist_re, cos_inner, precision=hp) + jnp.einsum(
        "bkq,qm->bkm", twist_im, sin_inner, precision=hp
    )
    spec_im = jnp.einsum("bkq,qm->bkm", twist_im, cos_inner, precision=hp) - jnp.einsum(
        "bkq,qm->bkm", twist_re, sin_inner, precision=hp
    )
    wave = outer_index[:, None] + outer * inner_index[None, :]
    folded = jnp.minimum(wave, length - wave)
    filt = (3 * folded < length).astype(jnp.float32)
    phase = jnp.remainder(wave * shift_value, length).astype(jnp.float32) * (2.0 * math.pi / length)
    gain_re = filt * jnp.cos(phase)
    gain_im = -filt * jnp.sin(phase)
    mixed_re = spec_re * gain_re - spec_im * gain_im
    mixed_im = spec_re * gain_im + spec_im * gain_re
    back_re = jnp.einsum("bkm,qm->bkq", mixed_re, cos_inner, precision=hp) - jnp.einsum(
        "bkm,qm->bkq", mixed_im, sin_inner, precision=hp
    )
    back_im = jnp.einsum("bkm,qm->bkq", mixed_im, cos_inner, precision=hp) + jnp.einsum(
        "bkm,qm->bkq", mixed_re, sin_inner, precision=hp
    )
    turn_re = back_re * cos_twist - back_im * sin_twist
    turn_im = back_im * cos_twist + back_re * sin_twist
    result = jnp.einsum("bkq,pk->bpq", turn_re, cos_outer, precision=hp) - jnp.einsum(
        "bkq,pk->bpq", turn_im, sin_outer, precision=hp
    )
    return (result / length).reshape(count, length)


def on_device(cycle, field, shift, owner):
    layers, variables, radial, sector = cycle.shape
    stacked = cycle.reshape(layers * variables, radial, sector)
    shift_value = shift[0]
    piece = lax.all_to_all(stacked, "az", split_axis=1, concat_axis=2, tiled=True)
    moved = spectral_shift(piece.reshape(-1, piece.shape[2]), shift_value).reshape(piece.shape)
    shifted_flat = lax.all_to_all(moved, "az", split_axis=2, concat_axis=1, tiled=True)
    shifted_cycle = shifted_flat.reshape(layers, variables, radial, sector)
    weights = jnp.array(LAYER_WEIGHTS, jnp.float32)
    depth, count, rows, width = shifted_cycle.shape
    grouped = shifted_cycle.reshape(depth, count, rows // KR, KR, width)
    ghost = lax.all_gather(
        jnp.einsum("l,lvrkt->vrt", weights, grouped, precision=lax.Precision.HIGHEST) / KR,
        "ax",
        axis=1,
        tiled=True,
    )
    mask = owner.astype(jnp.float32)[None, :, :, None]
    speeds = jnp.array(AXIAL_SPEEDS, jnp.float32)[:, None, None, None]
    at_inlet = lax.axis_index("ax") == 0

    def rates(state):
        radial_pad = padded(state, (("rad", 1),), 1)
        axial_pad = padded(state, (("ax", 2),), 1)
        lower = jnp.where(at_inlet, ghost, axial_pad[:, :, 0])
        outward = radial_pad[:, 2:]
        inward = radial_pad[:, :-2]
        above = axial_pad[:, :, 2:]
        below = jnp.concatenate([lower[:, :, None], axial_pad[:, :, 1:-2]], axis=2)
        return mask * (
            DIFFUSION * (outward + inward + above + below - 4.0 * state)
            - 0.5 * speeds * (above - below)
            - 0.5 * SWIRL_SPEED * (outward - inward)
        )

    first = rates(field)
    second = rates(field + 0.5 * first)
    third = rates(field + 0.5 * second)
    fourth = rates(field + third)
    field_next = field + (first + 2.0 * second + 2.0 * third + fourth) / 6.0
    return (field_next, shifted_cycle)


def solution(mesh):
    in_specs = (P(None, None, ("rad", "ax"), "az"), P(None, "rad", "ax", "az"), P(), P("rad", "ax"))
    out_specs = (P(None, "rad", "ax", "az"), P(None, None, ("rad", "ax"), "az"))
    return jax.shard_map(
        on_device, mesh=mesh, in_specs=in_specs, out_specs=out_specs, check_vma=False
    )
```

profile of v0, /device:TPU:1, one launch (start us, length us, event | category | flops | bytes accessed | tf_op | source)
XLA Modules:
  0.0 716.4 jit_solution(15796967327889109579)
XLA Ops:
  0.6 8.2 %copy.187 = f32[20,64,1024]{2,0,1:T(8,128)} copy(f32[20,64,1024]{2,1,0:T(8,128)} %bitcast.97) | data formatting | bytes 10485760 | tf_op jit(solution)/shard_map/reshape | solution.py:79
  8.8 5.6 all-to-all-start
  15.6 137.3 %all-to-all-done = f32[20,64,1024]{2,0,1:T(8,128)} async-done(((f32[20,64,1024]{2,0,1:T(8,128)}), f32[20,64,1024]{2,0,1:T(8,128)}, u32[]{:S(2)}, u32[]{:S(2)}) %all-to-all-start) | async-done | bytes 5242912 | tf_op jit(solution)/shard_map/all_to_all | solution.py:81
  152.9 8.5 %copy.189 = f32[20,16,4,1024]{3,2,1,0:T(4,128)} copy(f32[20,16,4,1024]{3,0,1,2:T(8,128)} %bitcast.5) | data formatting | bytes 10485760 | tf_op jit(solution)/shard_map/all_to_all | solution.py:81
  161.4 9.6 %reshape_reshape.9 = f32[320,64,64]{2,1,0:T(8,128)} reshape(f32[20,16,4,1024]{3,2,1,0:T(4,128)} %copy.189) | data formatting | bytes 10485760 | tf_op jit(solution)/shard_map/reshape;reshape | solution.py:44
  171.1 11.8 %copy.191 = f32[320,64,64]{0,1,2:T(8,128)} copy(f32[320,64,64]{2,1,0:T(8,128)} %reshape_reshape.9) | data formatting | bytes 10485760 | tf_op jit(solution)/shard_map/reshape;reshape | solution.py:44
  182.9 8.7 %fusion.44 = f32[64,320,64]{1,0,2:T(8,128)S(1)} fusion(f32[320,64,64]{0,1,2:T(8,128)} %copy.191), kind=kOutput, calls=%fused_computation.85 | convolution fusion | flops 1006690304 | bytes 10485760 | tf_op jit(solution)/shard_map/bpq,pk->bkq/dot_general | solution.py:46
  191.6 7.6 %add_bitcast_fusion = (f32[320,64,64]{0,1,2:T(8,128)S(1)}, f32[320,64,64]{0,1,2:T(8,128)S(1)}) fusion(f32[64,320,64]{1,0,2:T(8,128)S(1)} %fusion.44, f32[64,64]{0,1:T(8,128)S(1)} %copy.195, f32[64,64]{0,1:T(8,128)S(1)} %copy.192, f32[320,64,64]{0,1,2:T(8,128)S(1)} %copy-done.2), kind=kOutput, calls=%fused_computation.10 | convolution fusion | flops 1015865344 | bytes 21004288 | tf_op jit(solution)/shard_map/bpq,pk->bkq/dot_general | solution.py:45
  199.2 14.0 %fusion.10 = f32[320,64,64]{0,2,1:T(8,128)} fusion(f32[320,64,64]{0,1,2:T(8,128)S(1)} %get-tuple-element.16), kind=kOutput, calls=%fused_computation.17 | convolution fusion | flops 1006690304 | bytes 10485760 | tf_op jit(solution)/shard_map/bkq,qm->bkm/dot_general | solution.py:49
  213.2 13.2 %fusion.8 = f32[320,64,64]{0,2,1:T(8,128)} fusion(f32[320,64,64]{0,1,2:T(8,128)S(1)} %get-tuple-element.16), kind=kOutput, calls=%fused_computation.15 | convolution fusion | flops 1006690304 | bytes 10485760 | tf_op jit(solution)/shard_map/bkq,qm->bkm/dot_general | solution.py:52
  226.4 13.3 %fusion.6 = f32[320,64,64]{0,2,1:T(8,128)} fusion(f32[320,64,64]{0,1,2:T(8,128)S(1)} %get-tuple-element.17), kind=kOutput, calls=%fused_computation.13 | convolution fusion | flops 1006690304 | bytes 10485760 | tf_op jit(solution)/shard_map/bkq,qm->bkm/dot_general | solution.py:49
  239.7 19.1 %multiply_subtract_fusion.1 = (f32[320,64,64]{0,2,1:T(8,128)}, f32[320,64,64]{0,2,1:T(8,128)S(1)}) fusion(f32[64,64]{1,0:T(8,128)S(1)} %get-tuple-element.35, f32[64,64]{1,0:T(8,128)S(1)} %get-tuple-element.34, f32[320,64,64]{0,2,1:T(8,128)} %fusion.8, f32[320,64,64]{0,2,1:T(8,128)} %fusion.10, f32[320,64,64]{0,2,1:T(8,128)} %fusion.6, ...), kind=kOutput, calls=%fused_computation.8 | convolution fusion | flops 1017176064 | bytes 31490048 | tf_op jit(solution)/shard_map/bkq,qm->bkm/dot_general | solution.py:52
  258.9 10.3 %fusion.38 = f32[320,64,64]{0,2,1:T(8,128)} fusion(f32[320,64,64]{0,2,1:T(8,128)} %get-tuple-element.14), kind=kOutput, calls=%fused_computation.79 | convolution fusion | flops 1006690304 | bytes 10485760 | tf_op jit(solution)/shard_map/bkm,qm->bkq/dot_general | solution.py:66
  269.2 7.8 %fusion.53 = f32[320,64,64]{0,2,1:T(8,128)} fusion(f32[320,64,64]{0,2,1:T(8,128)S(1)} %copy-done), kind=kOutput, calls=%fused_computation.94 | convolution fusion | flops 1006690304 | bytes 10485760 | tf_op jit(solution)/shard_map/bkm,qm->bkq/dot_general | solution.py:63
  277.0 7.9 %fusion.40 = f32[320,64,64]{0,2,1:T(8,128)} fusion(f32[320,64,64]{0,2,1:T(8,128)S(1)} %get-tuple-element.15), kind=kOutput, calls=%fused_computation.81 | convolution fusion | flops 1006690304 | bytes 10485760 | tf_op jit(solution)/shard_map/bkm,qm->bkq/dot_general | solution.py:63
  284.9 15.2 %multiply_subtract_fusion = (f32[320,64,64]{0,2,1:T(8,128)}, f32[320,64,64]{0,2,1:T(8,128)}) fusion(f32[64,64]{1,0:T(8,128)S(1)} %get-tuple-element.36, f32[64,64]{1,0:T(8,128)S(1)} %get-tuple-element.37, f32[320,64,64]{0,2,1:T(8,128)} %fusion.38, f32[320,64,64]{0,2,1:T(8,128)} %fusion.53, f32[320,64,64]{0,2,1:T(8,128)} %fusion.40, ...), kind=kOutput, calls=%fused_computation.6 | convolution fusion | flops 1017176064 | bytes 31490048 | tf_op jit(solution)/shard_map/bkm,qm->bkq/dot_general | solution.py:66
  300.1 12.4 %fusion = f32[64,320,64]{1,0,2:T(8,128)S(1)} fusion(f32[320,64,64]{0,2,1:T(8,128)} %get-tuple-element.13), kind=kOutput, calls=%fused_computation | convolution fusion | flops 1006690304 | bytes 10485760 | tf_op jit(solution)/shard_map/bkq,pk->bpq/dot_general | solution.py:71
  312.5 11.2 %multiply_bitcast_fusion = f32[320,64,64]{0,1,2:T(8,128)} fusion(f32[64,320,64]{1,0,2:T(8,128)S(1)} %fusion, f32[320,64,64]{0,2,1:T(8,128)S(1)} %copy-done.3), kind=kOutput, calls=%fused_computation.4 | convolution fusion | flops 1009311744 | bytes 15728640 | tf_op jit(solution)/shard_map/bkq,pk->bpq/dot_general | solution.py:71
  323.7 12.6 %copy.206 = f32[320,64,64]{2,1,0:T(8,128)} copy(f32[320,64,64]{0,1,2:T(8,128)} %multiply_bitcast_fusion) | data formatting | bytes 10485760 | tf_op jit(solution)/shard_map/div | solution.py:74
  336.2 9.7 %reshape_reshape.10 = f32[20,16,4096]{2,1,0:T(8,128)} reshape(f32[320,64,64]{2,1,0:T(8,128)} %copy.206) | data formatting | bytes 10485760 | tf_op jit(solution)/shard_map/reshape;reshape | solution.py:82
  346.0 18.7 %copy.207 = f32[20,16,4096]{0,1,2:T(8,128)} copy(f32[20,16,4096]{2,1,0:T(8,128)} %reshape_reshape.10) | data formatting | bytes 10485760 | tf_op jit(solution)/shard_map/reshape;reshape | solution.py:82
  364.7 56.1 %reshape.131 = f32[4,1,327680]{2,1,0:T(1,128)} reshape(f32[4096,16,20]{2,1,0:T(8,128)} %bitcast.92) | data formatting | bytes 10485760
  420.9 5.2 all-to-all-start.1
  427.5 4.3 collective-permute-start.3
  439.1 102.1 %all-to-all-done.1 = f32[4,1,327680]{2,1,0:T(1,128)} async-done(((f32[4,1,327680]{2,1,0:T(1,128)}), f32[4,1,327680]{2,1,0:T(1,128)}, u32[]{:S(2)}, u32[]{:S(2)}) %all-to-all-start.1) | async-done | bytes 5242912 | tf_op jit(solution)/shard_map/all_to_all | solution.py:83
  541.8 18.3 %reduce = f32[4,327680]{1,0:T(4,128)} reduce(f32[4,1,327680]{2,1,0:T(1,128)} %all-to-all-done.1, f32[]{:T(128)} %broadcast.363), dimensions={1}, to_apply=%all_to_all.25.reduce_sub_computation | reduce | bytes 10485764 | tf_op jit(solution)/shard_map/all_to_all | solution.py:83
  560.1 52.9 %reshape.132 = f32[4096,16,20]{2,1,0:T(8,128)} reshape(f32[4,327680]{1,0:T(4,128)} %reduce) | data formatting | bytes 10485760
  613.0 22.4 %copy.234 = f32[20,16,4,1024]{3,2,1,0:T(4,128)} copy(f32[20,16,4,1024]{0,1,3,2:T(8,128)} %bitcast.93) | data formatting | bytes 10485760 | tf_op jit(solution)/shard_map/all_to_all | solution.py:83
  635.4 9.2 %copy.209 = f32[20,4,16,1024]{3,2,1,0:T(8,128)} copy(f32[20,4,16,1024]{3,1,2,0:T(4,128)} %bitcast.94) | data formatting | bytes 10485760 | tf_op jit(solution)/shard_map/all_to_all | solution.py:83
  644.6 4.6 reduce_sum.9
  651.9 9.0 %all_gather.3 = f32[5,32,1024]{2,1,0:T(8,128)S(1)} all-gather(f32[5,8,1024]{2,1,0:T(8,128)S(1)} %bitcast_multiply_fusion), channel_id=1, replica_groups=mesh['az'=4,'rad'=2,'ax'=4] {'ax'}, dimensions={1}, use_global_device_ids=true | all-gather | bytes 819200 | tf_op jit(solution)/shard_map/all_gather | solution.py:88
  708.6 5.5 multiply_add_fusion.2
  (75 shorter events, 62.1 us)
Async XLA Ops:
  8.8 144.1 %all-to-all-start = ((f32[20,64,1024]{2,0,1:T(8,128)}), f32[20,64,1024]{2,0,1:T(8,128)}, u32[]{:S(2)}, u32[]{:S(2)}) async-start(f32[20,64,1024]{2,0,1:T(8,128)} %copy.187), calls=%async_computation | async-start | bytes 12582912 | tf_op jit(solution)/shard_map/all_to_all | solution.py:81
  182.9 8.7 %copy-start.2 = (f32[320,64,64]{0,1,2:T(8,128)S(1)}, f32[320,64,64]{0,1,2:T(8,128)}, u32[]{:S(2)}) copy-start(f32[320,64,64]{0,1,2:T(8,128)} %copy.191) | copy-start | bytes 15728644
  199.2 27.2 %copy-start.1 = (f32[320,64,64]{0,1,2:T(8,128)}, f32[320,64,64]{0,1,2:T(8,128)S(1)}, u32[]{:S(2)}) copy-start(f32[320,64,64]{0,1,2:T(8,128)S(1)} %get-tuple-element.17) | copy-start | bytes 15728644
  258.9 10.3 %copy-start = (f32[320,64,64]{0,2,1:T(8,128)S(1)}, f32[320,64,64]{0,2,1:T(8,128)}, u32[]{:S(2)}) copy-start(f32[320,64,64]{0,2,1:T(8,128)} %get-tuple-element.14) | copy-start | bytes 15728644
  300.1 12.4 %copy-start.3 = (f32[320,64,64]{0,2,1:T(8,128)S(1)}, f32[320,64,64]{0,2,1:T(8,128)}, u32[]{:S(2)}) copy-start(f32[320,64,64]{0,2,1:T(8,128)} %get-tuple-element.12) | copy-start | bytes 15728644
  420.9 5.2 copy-start.4
  420.9 120.3 %all-to-all-start.1 = ((f32[4,1,327680]{2,1,0:T(1,128)}), f32[4,1,327680]{2,1,0:T(1,128)}, u32[]{:S(2)}, u32[]{:S(2)}) async-start(f32[4,1,327680]{2,1,0:T(1,128)} %reshape.131), calls=%async_computation.1 | async-start | bytes 10485760 | tf_op jit(solution)/shard_map/all_to_all | solution.py:83
  426.5 12.6 %copy-start.6 = (s32[32,2]{0,1:T(2,128)S(1)}, s32[32,2]{0,1:T(2,128)}, u32[]{:S(2)}) copy-start(s32[32,2]{0,1:T(2,128)} %param.9) | copy-start | bytes 772
  427.5 233.4 %collective-permute-start.3 = (f32[5,32,1,1024]{3,1,0,2:T(8,128)}, f32[5,32,1,1024]{3,1,0,2:T(8,128)}, u32[]{:S(2)}, u32[]{:S(2)}) collective-permute-start(f32[5,32,1,1024]{3,1,0,2:T(8,128)} %get-tuple-element.30), channel_id=1, source_target_pairs={{0,1},{1,2},{2,3},{4,5},{5,6},{6,7},{8,9},{9,10},{10,11},{12,13},{... | collective-permute-start | bytes 1966088 | tf_op jit(solution)/shard_map/ppermute | solution.py:21
  431.8 230.3 %collective-permute-start.2 = (f32[5,32,1,1024]{3,1,0,2:T(8,128)S(1)}, f32[5,32,1,1024]{3,1,0,2:T(8,128)}, u32[]{:S(2)}, u32[]{:S(2)}) collective-permute-start(f32[5,32,1,1024]{3,1,0,2:T(8,128)S(1)} %get-tuple-element.31), channel_id=1, source_target_pairs={{1,0},{2,1},{3,2},{5,4},{6,5},{7,6},{9,8},{10,9},{11,10},{13,12},{... | collective-permute-start | bytes 1966088 | tf_op jit(solution)/shard_map/ppermute | solution.py:22
  433.8 228.3 %collective-permute-start = (f32[5,1,2,1024]{3,1,0,2:T(1,128)S(1)}, f32[5,1,2,1024]{3,1,0,2:T(1,128)S(1)}, u32[]{:S(2)}, u32[]{:S(2)}) collective-permute-start(f32[5,1,2,1024]{3,1,0,2:T(1,128)S(1)} %copy.181), channel_id=1, source_target_pairs={{4,0},{5,1},{6,2},{7,3},{12,8},{13,9},{14,10},{15,11},{20,16},{21,... | collective-permute-start | bytes 122888 | tf_op jit(solution)/shard_map/ppermute | solution.py:22
  435.1 227.0 %collective-permute-start.1 = (f32[5,1,2,1024]{3,1,0,2:T(1,128)S(1)}, f32[5,1,2,1024]{3,1,0,2:T(1,128)S(1)}, u32[]{:S(2)}, u32[]{:S(2)}) collective-permute-start(f32[5,1,2,1024]{3,1,0,2:T(1,128)S(1)} %copy.183), channel_id=1, source_target_pairs={{0,4},{1,5},{2,6},{3,7},{8,12},{9,13},{10,14},{11,15},{16,20},{17,... | collective-permute-start | bytes 122888 | tf_op jit(solution)/shard_map/ppermute | solution.py:21
  644.6 4.6 copy-start.7
  651.9 10.2 %copy-start.5 = (f32[5]{0:T(128)S(1)}, f32[5]{0:T(128)}, u32[]{:S(2)}) copy-start(f32[5]{0:T(128)} %constant.78) | copy-start | bytes 64
  664.2 9.9 %collective-permute-start.7 = (f32[5,32,1,1024]{3,1,0,2:T(8,128)S(1)}, f32[5,32,1,1024]{3,1,0,2:T(8,128)S(1)}, u32[]{:S(2)}, u32[]{:S(2)}) collective-permute-start(f32[5,32,1,1024]{3,1,0,2:T(8,128)S(1)} %get-tuple-element.28), channel_id=1, source_target_pairs={{0,1},{1,2},{2,3},{4,5},{5,6},{6,7},{8,9},{9,10},{10,11},{12,13},{... | collective-permute-start | bytes 1966088 | tf_op jit(solution)/shard_map/ppermute | solution.py:21
  666.7 11.9 %collective-permute-start.6 = (f32[5,32,1,1024]{3,1,0,2:T(8,128)S(1)}, f32[5,32,1,1024]{3,1,0,2:T(8,128)S(1)}, u32[]{:S(2)}, u32[]{:S(2)}) collective-permute-start(f32[5,32,1,1024]{3,1,0,2:T(8,128)S(1)} %get-tuple-element.29), channel_id=1, source_target_pairs={{1,0},{2,1},{3,2},{5,4},{6,5},{7,6},{9,8},{10,9},{11,10},{13,12},{... | collective-permute-start | bytes 1966088 | tf_op jit(solution)/shard_map/ppermute | solution.py:22
  668.7 5.6 collective-permute-start.4
  670.0 5.2 collective-permute-start.5
  679.8 10.0 %collective-permute-start.11 = (f32[5,32,1,1024]{3,1,0,2:T(8,128)S(1)}, f32[5,32,1,1024]{3,1,0,2:T(8,128)S(1)}, u32[]{:S(2)}, u32[]{:S(2)}) collective-permute-start(f32[5,32,1,1024]{3,1,0,2:T(8,128)S(1)} %get-tuple-element.24), channel_id=1, source_target_pairs={{0,1},{1,2},{2,3},{4,5},{5,6},{6,7},{8,9},{9,10},{10,11},{12,13},{... | collective-permute-start | bytes 1966088 | tf_op jit(solution)/shard_map/ppermute | solution.py:21
  681.7 11.9 %collective-permute-start.10 = (f32[5,32,1,1024]{3,1,0,2:T(8,128)S(1)}, f32[5,32,1,1024]{3,1,0,2:T(8,128)S(1)}, u32[]{:S(2)}, u32[]{:S(2)}) collective-permute-start(f32[5,32,1,1024]{3,1,0,2:T(8,128)S(1)} %get-tuple-element.25), channel_id=1, source_target_pairs={{1,0},{2,1},{3,2},{5,4},{6,5},{7,6},{9,8},{10,9},{11,10},{13,12},{... | collective-permute-start | bytes 1966088 | tf_op jit(solution)/shard_map/ppermute | solution.py:22
  684.2 5.7 collective-permute-start.8
  685.5 5.2 collective-permute-start.9
  694.8 9.7 %collective-permute-start.15 = (f32[5,32,1,1024]{3,1,0,2:T(8,128)S(1)}, f32[5,32,1,1024]{3,1,0,2:T(8,128)S(1)}, u32[]{:S(2)}, u32[]{:S(2)}) collective-permute-start(f32[5,32,1,1024]{3,1,0,2:T(8,128)S(1)} %get-tuple-element.20), channel_id=1, source_target_pairs={{0,1},{1,2},{2,3},{4,5},{5,6},{6,7},{8,9},{9,10},{10,11},{12,13},{... | collective-permute-start | bytes 1966088 | tf_op jit(solution)/shard_map/ppermute | solution.py:21
  696.7 11.9 %collective-permute-start.14 = (f32[5,32,1,1024]{3,1,0,2:T(8,128)S(1)}, f32[5,32,1,1024]{3,1,0,2:T(8,128)S(1)}, u32[]{:S(2)}, u32[]{:S(2)}) collective-permute-start(f32[5,32,1,1024]{3,1,0,2:T(8,128)S(1)} %get-tuple-element.21), channel_id=1, source_target_pairs={{1,0},{2,1},{3,2},{5,4},{6,5},{7,6},{9,8},{10,9},{11,10},{13,12},{... | collective-permute-start | bytes 1966088 | tf_op jit(solution)/shard_map/ppermute | solution.py:22
  699.2 5.4 collective-permute-start.12
  700.5 5.2 collective-permute-start.13
where the time goes:
time: 722 us; the launch traced here: 716 us
  waiting for transfers between devices  252 us (35%)
  local copies, waits for them, and re-layouts  225 us (31%)
  matrix products  143 us (20%)
  starting transfers between devices  51.5 us (7%)
  other arithmetic  34.3 us (5%)
  blocking collectives  8.99 us (1%)
    all_to_all x1, waiting for transfers between devices, on_device(): lax.all_to_all(stacked, 'az', split_axis=1, concat_axis=2, tiled=True)  137 us
    unnamed x20, local copies, waits for them, and re-layouts  112 us
    all_to_all x1, waiting for transfers between devices, on_device(): lax.all_to_all(moved, 'az', split_axis=2, concat_axis=1, tiled=True)  102 us
    all_to_all x3, local copies, waits for them, and re-layouts, on_device(): lax.all_to_all(moved, 'az', split_axis=2, concat_axis=1, tiled=True)  32.1 us
    another operation x2, local copies, waits for them, and re-layouts, on_device(): spectral_shift(piece.reshape(-1, piece.shape[2]), shift_value)  28.5 us
    ppermute x8, starting transfers between devices, padded(): before = lax.ppermute(last, axis, up)  26.7 us
    another operation x2, local copies, waits for them, and re-layouts, spectral_shift(): grid = rows.reshape(count, outer, inner)  21.5 us
    dot_general x1, matrix products, spectral_shift(): jnp.einsum('bkq,qm->bkm', twist_im, cos_inner, precision=hp)  19.1 us
  transfers between devices with their start and end apart: 18, of which 9 were waited for; matrix products, arithmetic and copies ran while one was open for 16% of the time, Pallas kernels for 0%

commit v1 on v0

--- a/solution.py
+++ b/solution.py
@@ -80,7 +80,19 @@
     shift_value = shift[0]
     piece = lax.all_to_all(stacked, "az", split_axis=1, concat_axis=2, tiled=True)
     moved = spectral_shift(piece.reshape(-1, piece.shape[2]), shift_value).reshape(piece.shape)
-    shifted_flat = lax.all_to_all(moved, "az", split_axis=2, concat_axis=1, tiled=True)
+    ways, here = (lax.axis_size("az"), lax.axis_index("az"))
+    width_2 = moved.shape[2] // ways
+    shape = list(moved.shape)
+    shape[2] = width_2
+    height = shape[1]
+    shape[1] = height * ways
+    full = jnp.zeros(shape, moved.dtype)
+    for mask_2 in range(ways):
+        part = lax.dynamic_slice_in_dim(moved, (here ^ mask_2) * width_2, width_2, axis=2)
+        if mask_2:
+            part = lax.ppermute(part, "az", [(d, d ^ mask_2) for d in range(ways)])
+        full = lax.dynamic_update_slice_in_dim(full, part, (here ^ mask_2) * height, axis=1)
+    shifted_flat = full
     shifted_cycle = shifted_flat.reshape(layers, variables, radial, sector)
     weights = jnp.array(LAYER_WEIGHTS, jnp.float32)
     depth, count, rows, width = shifted_cycle.shape

time: 722 us -> 547 us (0.76)
  the two profiles are of different devices: /device:TPU:1 before, /device:TPU:9 now
where the time goes in v1:
time: 547 us; the launch traced here: 542 us
  waiting for transfers between devices  215 us (39%)
  matrix products  143 us (26%)
  local copies, waits for them, and re-layouts  79.3 us (14%)
  starting transfers between devices  76.1 us (14%)
  other arithmetic  15.9 us (3%)
  blocking collectives  9.72 us (2%)
    all_to_all x1, waiting for transfers between devices, on_device(): lax.all_to_all(stacked, 'az', split_axis=1, concat_axis=2, tiled=True)  134 us
    ppermute x3, waiting for transfers between devices, on_device(): part = lax.ppermute(part, 'az', [(d, d ^ mask_2) for d in range(ways)])  66.7 us
    ppermute x8, starting transfers between devices, padded(): before = lax.ppermute(last, axis, up)  50.6 us
    another operation x2, local copies, waits for them, and re-layouts, spectral_shift(): grid = rows.reshape(count, outer, inner)  21.4 us
    dot_general x1, matrix products, spectral_shift(): jnp.einsum('bkq,qm->bkm', twist_im, cos_inner, precision=hp)  19.1 us
    ppermute x8, starting transfers between devices, padded(): after = lax.ppermute(leading, axis, down)  15.2 us
    dot_general x1, matrix products, spectral_shift(): jnp.einsum('bkm,qm->bkq', mixed_im, cos_inner, precision=hp)  15 us
    dot_general x1, matrix products, spectral_shift(): jnp.einsum('bkq,qm->bkm', twist_re, sin_inner, precision=hp)  13.8 us
  transfers between devices with their start and end apart: 20, of which 11 were waited for; matrix products, arithmetic and copies ran while one was open for 3% of the time, Pallas kernels for 0%

profile of v1, /device:TPU:9, one launch (start us, length us, event | category | flops | bytes accessed | tf_op | source)
XLA Modules:
  0.0 541.9 jit_solution(9781264295532800191)
XLA Ops:
  0.6 8.2 %copy.144 = f32[20,64,1024]{2,0,1:T(8,128)} copy(f32[20,64,1024]{2,1,0:T(8,128)} %bitcast.88) | data formatting | bytes 10485760 | tf_op jit(solution)/shard_map/reshape | solution.py:79
  8.9 5.8 %all-to-all-start = ((f32[20,64,1024]{2,0,1:T(8,128)}), f32[20,64,1024]{2,0,1:T(8,128)}, u32[]{:S(2)}, u32[]{:S(2)}) async-start(f32[20,64,1024]{2,0,1:T(8,128)} %copy.144), calls=%async_computation | async-start | bytes 12582912 | tf_op jit(solution)/shard_map/all_to_all | solution.py:81
  15.8 133.5 %all-to-all-done = f32[20,64,1024]{2,0,1:T(8,128)} async-done(((f32[20,64,1024]{2,0,1:T(8,128)}), f32[20,64,1024]{2,0,1:T(8,128)}, u32[]{:S(2)}, u32[]{:S(2)}) %all-to-all-start) | async-done | bytes 5242912 | tf_op jit(solution)/shard_map/all_to_all | solution.py:81
  149.3 8.5 %copy.146 = f32[20,16,4,1024]{3,2,1,0:T(4,128)} copy(f32[20,16,4,1024]{3,0,1,2:T(8,128)} %bitcast.5) | data formatting | bytes 10485760 | tf_op jit(solution)/shard_map/all_to_all | solution.py:81
  157.8 9.6 %reshape_reshape.9 = f32[320,64,64]{2,1,0:T(8,128)} reshape(f32[20,16,4,1024]{3,2,1,0:T(4,128)} %copy.146) | data formatting | bytes 10485760 | tf_op jit(solution)/shard_map/reshape;reshape | solution.py:44
  167.4 11.8 %copy.148 = f32[320,64,64]{0,1,2:T(8,128)} copy(f32[320,64,64]{2,1,0:T(8,128)} %reshape_reshape.9) | data formatting | bytes 10485760 | tf_op jit(solution)/shard_map/reshape;reshape | solution.py:44
  179.2 8.7 %fusion.44 = f32[64,320,64]{1,0,2:T(8,128)S(1)} fusion(f32[320,64,64]{0,1,2:T(8,128)} %copy.148), kind=kOutput, calls=%fused_computation.86 | convolution fusion | flops 1006690304 | bytes 10485760 | tf_op jit(solution)/shard_map/bpq,pk->bkq/dot_general | solution.py:46
  187.9 7.6 %add_bitcast_fusion = (f32[320,64,64]{0,1,2:T(8,128)S(1)}, f32[320,64,64]{0,1,2:T(8,128)S(1)}) fusion(f32[64,320,64]{1,0,2:T(8,128)S(1)} %fusion.44, f32[64,64]{0,1:T(8,128)S(1)} %copy.152, f32[64,64]{0,1:T(8,128)S(1)} %copy.149, f32[320,64,64]{0,1,2:T(8,128)S(1)} %copy-done.2), kind=kOutput, calls=%fused_computation.10 | convolution fusion | flops 1015865344 | bytes 21004288 | tf_op jit(solution)/shard_map/bpq,pk->bkq/dot_general | solution.py:45
  195.6 13.8 %fusion.8 = f32[320,64,64]{0,2,1:T(8,128)} fusion(f32[320,64,64]{0,1,2:T(8,128)S(1)} %get-tuple-element.14), kind=kOutput, calls=%fused_computation.15 | convolution fusion | flops 1006690304 | bytes 10485760 | tf_op jit(solution)/shard_map/bkq,qm->bkm/dot_general | solution.py:52
  209.4 13.2 %fusion.10 = f32[320,64,64]{0,2,1:T(8,128)} fusion(f32[320,64,64]{0,1,2:T(8,128)S(1)} %get-tuple-element.14), kind=kOutput, calls=%fused_computation.17 | convolution fusion | flops 1006690304 | bytes 10485760 | tf_op jit(solution)/shard_map/bkq,qm->bkm/dot_general | solution.py:49
  222.6 13.5 %fusion.6 = f32[320,64,64]{0,2,1:T(8,128)} fusion(f32[320,64,64]{0,1,2:T(8,128)S(1)} %get-tuple-element.15), kind=kOutput, calls=%fused_computation.13 | convolution fusion | flops 1006690304 | bytes 10485760 | tf_op jit(solution)/shard_map/bkq,qm->bkm/dot_general | solution.py:49
  236.1 19.1 %multiply_subtract_fusion.1 = (f32[320,64,64]{0,2,1:T(8,128)}, f32[320,64,64]{0,2,1:T(8,128)S(1)}) fusion(f32[64,64]{1,0:T(8,128)S(1)} %get-tuple-element.37, f32[64,64]{1,0:T(8,128)S(1)} %get-tuple-element.36, f32[320,64,64]{0,2,1:T(8,128)} %fusion.8, f32[320,64,64]{0,2,1:T(8,128)} %fusion.10, f32[320,64,64]{0,2,1:T(8,128)} %fusion.6, ...), kind=kOutput, calls=%fused_computation.8 | convolution fusion | flops 1017176064 | bytes 31490048 | tf_op jit(solution)/shard_map/bkq,qm->bkm/dot_general | solution.py:52
  255.3 10.2 %fusion.38 = f32[320,64,64]{0,2,1:T(8,128)} fusion(f32[320,64,64]{0,2,1:T(8,128)} %get-tuple-element.12), kind=kOutput, calls=%fused_computation.80 | convolution fusion | flops 1006690304 | bytes 10485760 | tf_op jit(solution)/shard_map/bkm,qm->bkq/dot_general | solution.py:66
  265.5 7.8 %fusion.53 = f32[320,64,64]{0,2,1:T(8,128)} fusion(f32[320,64,64]{0,2,1:T(8,128)S(1)} %copy-done), kind=kOutput, calls=%fused_computation.95 | convolution fusion | flops 1006690304 | bytes 10485760 | tf_op jit(solution)/shard_map/bkm,qm->bkq/dot_general | solution.py:63
  273.3 7.9 %fusion.40 = f32[320,64,64]{0,2,1:T(8,128)} fusion(f32[320,64,64]{0,2,1:T(8,128)S(1)} %get-tuple-element.13), kind=kOutput, calls=%fused_computation.82 | convolution fusion | flops 1006690304 | bytes 10485760 | tf_op jit(solution)/shard_map/bkm,qm->bkq/dot_general | solution.py:63
  281.2 15.0 %multiply_subtract_fusion = (f32[320,64,64]{0,2,1:T(8,128)}, f32[320,64,64]{0,2,1:T(8,128)}) fusion(f32[64,64]{1,0:T(8,128)S(1)} %get-tuple-element.38, f32[64,64]{1,0:T(8,128)S(1)} %get-tuple-element.39, f32[320,64,64]{0,2,1:T(8,128)} %fusion.38, f32[320,64,64]{0,2,1:T(8,128)} %fusion.53, f32[320,64,64]{0,2,1:T(8,128)} %fusion.40, ...), kind=kOutput, calls=%fused_computation.6 | convolution fusion | flops 1017176064 | bytes 31490048 | tf_op jit(solution)/shard_map/bkm,qm->bkq/dot_general | solution.py:66
  296.2 12.4 %fusion = f32[64,320,64]{1,0,2:T(8,128)S(1)} fusion(f32[320,64,64]{0,2,1:T(8,128)} %get-tuple-element.11), kind=kOutput, calls=%fused_computation | convolution fusion | flops 1006690304 | bytes 10485760 | tf_op jit(solution)/shard_map/bkq,pk->bpq/dot_general | solution.py:71
  308.6 11.5 %multiply_bitcast_fusion = f32[320,64,64]{0,1,2:T(8,128)} fusion(f32[64,320,64]{1,0,2:T(8,128)S(1)} %fusion, f32[320,64,64]{0,2,1:T(8,128)S(1)} %copy-done.3), kind=kOutput, calls=%fused_computation.4 | convolution fusion | flops 1009311744 | bytes 15728640 | tf_op jit(solution)/shard_map/bkq,pk->bpq/dot_general | solution.py:71
  320.1 12.5 %copy.163 = f32[320,64,64]{2,1,0:T(8,128)} copy(f32[320,64,64]{0,1,2:T(8,128)} %multiply_bitcast_fusion) | data formatting | bytes 10485760 | tf_op jit(solution)/shard_map/div | solution.py:74
  332.6 9.7 %reshape_reshape.10 = f32[20,16,4096]{2,1,0:T(8,128)} reshape(f32[320,64,64]{2,1,0:T(8,128)} %copy.163) | data formatting | bytes 10485760 | tf_op jit(solution)/shard_map/reshape;reshape | solution.py:82
  342.3 3.3 broadcast_in_dim.10
  349.3 3.3 collective-permute-start.3
  355.2 4.0 collective-permute-start.1
  360.6 46.4 %collective-permute-done.3 = f32[20,16,1024]{2,1,0:T(8,128)} collective-permute-done((f32[20,16,1024]{2,1,0:T(8,128)}, f32[20,16,1024]{2,1,0:T(8,128)}, u32[]{:S(2)}, u32[]{:S(2)}) %collective-permute-start.3) | collective-permute-done | bytes 1310752 | tf_op jit(solution)/shard_map/ppermute | solution.py:93
  407.0 3.6 collective-permute-start.2
  413.2 29.9 %collective-permute-start.6 = (f32[5,32,1,1024]{3,1,0,2:T(8,128)}, f32[5,32,1,1024]{3,1,0,2:T(8,128)}, u32[]{:S(2)}, u32[]{:S(2)}) collective-permute-start(f32[5,32,1,1024]{3,1,0,2:T(8,128)} %get-tuple-element.32), channel_id=1, source_target_pairs={{0,1},{1,2},{2,3},{4,5},{5,6},{6,7},{8,9},{9,10},{10,11},{12,13},{... | collective-permute-start | bytes 1966088 | tf_op jit(solution)/shard_map/ppermute | solution.py:21
  445.6 20.4 %collective-permute-done.5 = f32[20,16,1024]{2,1,0:T(8,128)} collective-permute-done((f32[20,16,1024]{2,1,0:T(8,128)}, f32[20,16,1024]{2,1,0:T(8,128)}, u32[]{:S(2)}, u32[]{:S(2)}) %collective-permute-start.5) | collective-permute-done | bytes 1310752 | tf_op jit(solution)/shard_map/ppermute | solution.py:93
  468.5 4.6 reduce_sum.9
  475.8 9.7 %all_gather.3 = f32[5,32,1024]{2,1,0:T(8,128)S(1)} all-gather(f32[5,8,1024]{2,1,0:T(8,128)S(1)} %bitcast_multiply_fusion), channel_id=1, replica_groups=mesh['az'=4,'rad'=2,'ax'=4] {'ax'}, dimensions={1}, use_global_device_ids=true | all-gather | bytes 819200 | tf_op jit(solution)/shard_map/all_gather | solution.py:100
  493.3 3.1 collective-permute-start.8
  526.1 4.0 collective-permute-start.16
  534.1 5.5 %multiply_add_fusion.2 = f32[5,32,2,1024]{3,1,0,2:T(8,128)S(1)} fusion(f32[5,32,2,1024]{3,1,0,2:T(8,128)S(1)} %copy.169, f32[5,32,2,1024]{3,1,0,2:T(8,128)S(1)} %copy_add_fusion, f32[5,32,1,1024]{3,1,0,2:T(8,128)S(1)} %get-tuple-element.23, f32[5,32,1,1024]{3,1,0,2:T(8,128)S(1)} %fusion.22, f32[5,32,1,1024]{3,1,0,2:T(8,128)S(1)} %collective-permute-done.17, ...), kind=kLoop, calls=%fused_computation.35 | loop fusion | flops 24576000 | bytes 14745876 | tf_op jit(solution)/shard_map/add | solution.py:128
  (79 shorter events, 61.8 us)
Async XLA Ops:
  8.9 140.4 %all-to-all-start = ((f32[20,64,1024]{2,0,1:T(8,128)}), f32[20,64,1024]{2,0,1:T(8,128)}, u32[]{:S(2)}, u32[]{:S(2)}) async-start(f32[20,64,1024]{2,0,1:T(8,128)} %copy.144), calls=%async_computation | async-start | bytes 12582912 | tf_op jit(solution)/shard_map/all_to_all | solution.py:81
  179.2 8.7 %copy-start.2 = (f32[320,64,64]{0,1,2:T(8,128)S(1)}, f32[320,64,64]{0,1,2:T(8,128)}, u32[]{:S(2)}) copy-start(f32[320,64,64]{0,1,2:T(8,128)} %copy.148) | copy-start | bytes 15728644
  195.5 27.0 %copy-start.1 = (f32[320,64,64]{0,1,2:T(8,128)}, f32[320,64,64]{0,1,2:T(8,128)S(1)}, u32[]{:S(2)}) copy-start(f32[320,64,64]{0,1,2:T(8,128)S(1)} %get-tuple-element.15) | copy-start | bytes 15728644
  255.2 10.3 %copy-start = (f32[320,64,64]{0,2,1:T(8,128)S(1)}, f32[320,64,64]{0,2,1:T(8,128)}, u32[]{:S(2)}) copy-start(f32[320,64,64]{0,2,1:T(8,128)} %get-tuple-element.12) | copy-start | bytes 15728644
  296.2 12.4 %copy-start.3 = (f32[320,64,64]{0,2,1:T(8,128)S(1)}, f32[320,64,64]{0,2,1:T(8,128)}, u32[]{:S(2)}) copy-start(f32[320,64,64]{0,2,1:T(8,128)} %get-tuple-element.10) | copy-start | bytes 15728644
  342.3 4.4 copy-start.4
  346.7 7.1 %copy-start.5 = (f32[5,32,2,1024]{3,2,1,0:T(2,128)S(1)}, f32[5,32,2,1024]{3,2,1,0:T(2,128)}, u32[]{:S(2)}) copy-start(f32[5,32,2,1024]{3,2,1,0:T(2,128)} %param.7) | copy-start | bytes 3932164
  349.3 57.7 %collective-permute-start.3 = (f32[20,16,1024]{2,1,0:T(8,128)}, f32[20,16,1024]{2,1,0:T(8,128)}, u32[]{:S(2)}, u32[]{:S(2)}) collective-permute-start(f32[20,16,1024]{2,1,0:T(8,128)} %get-tuple-element.18), channel_id=1, source_target_pairs={{0,8},{8,0},{16,24},{24,16},{1,9},{9,1},{17,25},{25,17},{2,10},{10... | collective-permute-start | bytes 3932168 | tf_op jit(solution)/shard_map/ppermute | solution.py:93
  352.6 60.6 %collective-permute-start.4 = (f32[20,16,1024]{2,1,0:T(8,128)}, f32[20,16,1024]{2,1,0:T(8,128)}, u32[]{:S(2)}, u32[]{:S(2)}) collective-permute-start(f32[20,16,1024]{2,1,0:T(8,128)} %get-tuple-element.17), channel_id=1, source_target_pairs={{0,16},{8,24},{16,0},{24,8},{1,17},{9,25},{17,1},{25,9},{2,18},{10... | collective-permute-start | bytes 3932168 | tf_op jit(solution)/shard_map/ppermute | solution.py:93
  352.6 113.4 %collective-permute-start.5 = (f32[20,16,1024]{2,1,0:T(8,128)}, f32[20,16,1024]{2,1,0:T(8,128)}, u32[]{:S(2)}, u32[]{:S(2)}) collective-permute-start(f32[20,16,1024]{2,1,0:T(8,128)} %get-tuple-element.16), channel_id=1, source_target_pairs={{0,24},{8,16},{16,8},{24,0},{1,25},{9,17},{17,9},{25,1},{2,26},{10... | collective-permute-start | bytes 3932168 | tf_op jit(solution)/shard_map/ppermute | solution.py:93
  353.8 132.9 %collective-permute-start = (f32[5,1,2,1024]{3,1,0,2:T(1,128)S(1)}, f32[5,1,2,1024]{3,1,0,2:T(1,128)S(1)}, u32[]{:S(2)}, u32[]{:S(2)}) collective-permute-start(f32[5,1,2,1024]{3,1,0,2:T(1,128)S(1)} %copy.138), channel_id=1, source_target_pairs={{4,0},{5,1},{6,2},{7,3},{12,8},{13,9},{14,10},{15,11},{20,16},{21,... | collective-permute-start | bytes 122888 | tf_op jit(solution)/shard_map/ppermute | solution.py:22
  355.2 4.5 copy-start.7
  355.2 131.6 %collective-permute-start.1 = (f32[5,1,2,1024]{3,1,0,2:T(1,128)S(1)}, f32[5,1,2,1024]{3,1,0,2:T(1,128)S(1)}, u32[]{:S(2)}, u32[]{:S(2)}) collective-permute-start(f32[5,1,2,1024]{3,1,0,2:T(1,128)S(1)} %copy.140), channel_id=1, source_target_pairs={{0,4},{1,5},{2,6},{3,7},{8,12},{9,13},{10,14},{11,15},{16,20},{17,... | collective-permute-start | bytes 122888 | tf_op jit(solution)/shard_map/ppermute | solution.py:21
  407.0 79.8 %collective-permute-start.2 = (f32[5,32,1,1024]{3,1,0,2:T(8,128)S(1)}, f32[5,32,1,1024]{3,1,0,2:T(8,128)}, u32[]{:S(2)}, u32[]{:S(2)}) collective-permute-start(f32[5,32,1,1024]{3,1,0,2:T(8,128)S(1)} %get-tuple-element.33), channel_id=1, source_target_pairs={{1,0},{2,1},{3,2},{5,4},{6,5},{7,6},{9,8},{10,9},{11,10},{13,12},{... | collective-permute-start | bytes 1966088 | tf_op jit(solution)/shard_map/ppermute | solution.py:22
  413.2 72.4 %collective-permute-start.6 = (f32[5,32,1,1024]{3,1,0,2:T(8,128)}, f32[5,32,1,1024]{3,1,0,2:T(8,128)}, u32[]{:S(2)}, u32[]{:S(2)}) collective-permute-start(f32[5,32,1,1024]{3,1,0,2:T(8,128)} %get-tuple-element.32), channel_id=1, source_target_pairs={{0,1},{1,2},{2,3},{4,5},{5,6},{6,7},{8,9},{9,10},{10,11},{12,13},{... | collective-permute-start | bytes 1966088 | tf_op jit(solution)/shard_map/ppermute | solution.py:21
  468.5 4.6 copy-start.8
  475.8 11.0 %copy-start.6 = (f32[5]{0:T(128)S(1)}, f32[5]{0:T(128)}, u32[]{:S(2)}) copy-start(f32[5]{0:T(128)} %constant.91) | copy-start | bytes 64
  488.9 9.9 %collective-permute-start.10 = (f32[5,32,1,1024]{3,1,0,2:T(8,128)S(1)}, f32[5,32,1,1024]{3,1,0,2:T(8,128)S(1)}, u32[]{:S(2)}, u32[]{:S(2)}) collective-permute-start(f32[5,32,1,1024]{3,1,0,2:T(8,128)S(1)} %get-tuple-element.30), channel_id=1, source_target_pairs={{0,1},{1,2},{2,3},{4,5},{5,6},{6,7},{8,9},{9,10},{10,11},{12,13},{... | collective-permute-start | bytes 1966088 | tf_op jit(solution)/shard_map/ppermute | solution.py:21
  491.3 11.9 %collective-permute-start.9 = (f32[5,32,1,1024]{3,1,0,2:T(8,128)S(1)}, f32[5,32,1,1024]{3,1,0,2:T(8,128)S(1)}, u32[]{:S(2)}, u32[]{:S(2)}) collective-permute-start(f32[5,32,1,1024]{3,1,0,2:T(8,128)S(1)} %get-tuple-element.31), channel_id=1, source_target_pairs={{1,0},{2,1},{3,2},{5,4},{6,5},{7,6},{9,8},{10,9},{11,10},{13,12},{... | collective-permute-start | bytes 1966088 | tf_op jit(solution)/shard_map/ppermute | solution.py:22
  493.3 5.5 %collective-permute-start.8 = (f32[5,1,2,1024]{3,1,0,2:T(1,128)S(1)}, f32[5,1,2,1024]{3,1,0,2:T(1,128)S(1)}, u32[]{:S(2)}, u32[]{:S(2)}) collective-permute-start(f32[5,1,2,1024]{3,1,0,2:T(1,128)S(1)} %get-tuple-element.29), channel_id=1, source_target_pairs={{0,4},{1,5},{2,6},{3,7},{8,12},{9,13},{10,14},{11,15},{16,20},{17,... | collective-permute-start | bytes 122888 | tf_op jit(solution)/shard_map/ppermute | solution.py:21
  496.4 5.4 collective-permute-start.7
  504.4 10.4 %collective-permute-start.14 = (f32[5,32,1,1024]{3,1,0,2:T(8,128)S(1)}, f32[5,32,1,1024]{3,1,0,2:T(8,128)S(1)}, u32[]{:S(2)}, u32[]{:S(2)}) collective-permute-start(f32[5,32,1,1024]{3,1,0,2:T(8,128)S(1)} %get-tuple-element.26), channel_id=1, source_target_pairs={{0,1},{1,2},{2,3},{4,5},{5,6},{6,7},{8,9},{9,10},{10,11},{12,13},{... | collective-permute-start | bytes 1966088 | tf_op jit(solution)/shard_map/ppermute | solution.py:21
  507.2 11.9 %collective-permute-start.13 = (f32[5,32,1,1024]{3,1,0,2:T(8,128)S(1)}, f32[5,32,1,1024]{3,1,0,2:T(8,128)S(1)}, u32[]{:S(2)}, u32[]{:S(2)}) collective-permute-start(f32[5,32,1,1024]{3,1,0,2:T(8,128)S(1)} %get-tuple-element.27), channel_id=1, source_target_pairs={{1,0},{2,1},{3,2},{5,4},{6,5},{7,6},{9,8},{10,9},{11,10},{13,12},{... | collective-permute-start | bytes 1966088 | tf_op jit(solution)/shard_map/ppermute | solution.py:22
  509.2 5.6 %collective-permute-start.12 = (f32[5,1,2,1024]{3,1,0,2:T(1,128)S(1)}, f32[5,1,2,1024]{3,1,0,2:T(1,128)S(1)}, u32[]{:S(2)}, u32[]{:S(2)}) collective-permute-start(f32[5,1,2,1024]{3,1,0,2:T(1,128)S(1)} %get-tuple-element.25), channel_id=1, source_target_pairs={{0,4},{1,5},{2,6},{3,7},{8,12},{9,13},{10,14},{11,15},{16,20},{17,... | collective-permute-start | bytes 122888 | tf_op jit(solution)/shard_map/ppermute | solution.py:21
  511.8 5.4 collective-permute-start.11
  520.3 9.7 %collective-permute-start.18 = (f32[5,32,1,1024]{3,1,0,2:T(8,128)S(1)}, f32[5,32,1,1024]{3,1,0,2:T(8,128)S(1)}, u32[]{:S(2)}, u32[]{:S(2)}) collective-permute-start(f32[5,32,1,1024]{3,1,0,2:T(8,128)S(1)} %get-tuple-element.22), channel_id=1, source_target_pairs={{0,1},{1,2},{2,3},{4,5},{5,6},{6,7},{8,9},{9,10},{10,11},{12,13},{... | collective-permute-start | bytes 1966088 | tf_op jit(solution)/shard_map/ppermute | solution.py:21
  522.2 11.9 %collective-permute-start.17 = (f32[5,32,1,1024]{3,1,0,2:T(8,128)S(1)}, f32[5,32,1,1024]{3,1,0,2:T(8,128)S(1)}, u32[]{:S(2)}, u32[]{:S(2)}) collective-permute-start(f32[5,32,1,1024]{3,1,0,2:T(8,128)S(1)} %get-tuple-element.23), channel_id=1, source_target_pairs={{1,0},{2,1},{3,2},{5,4},{6,5},{7,6},{9,8},{10,9},{11,10},{13,12},{... | collective-permute-start | bytes 1966088 | tf_op jit(solution)/shard_map/ppermute | solution.py:22
  524.8 5.4 collective-permute-start.15
  526.1 5.2 collective-permute-start.16
